TPU v7x, 256 devices: a whole 4x4x8 slice. The times are simulated.
256 devices in a mesh: space: 32 (over z_lo, y, core), dom: 8 (over z_hi, x).
Axes of the slice: x: 4, y: 4, z: 8 (z_hi: 2, z_lo: 4; z = z_hi * 4 + z_lo), core: 2. Of those that a mesh axis runs over, the one named last changes fastest.
Arguments:
- water_depth: float32 [16, 32, 256, 512], P('dom', 'space'), may hold values from 0 to 1.5
- infiltrated: float32 [16, 32, 256, 512], P('dom', 'space'), may hold values from 0.2 to 2
- terrain: float32 [32, 256, 512], P('space'), may hold values from -3 to 3
- land_mask: int32 [32, 256, 512], P('space'), may hold values from 0 to 1
- forcing: bfloat16 [2, 2, 32, 256, 512], P(None, None, 'space', 'dom'), may hold values from 0.049804688 to 1.5
- observed: bfloat16 [2, 32, 256, 512], P(None, 'space'), may hold values from 0 to 3.6
- conductivity: float32 [16], replicated, may hold values from 0.05 to 0.6
- suction: float32 [16], replicated, may hold values from 0.1 to 2
- manning: float32 [16], replicated, may hold values from 0.5 to 2
- assignment: int32 [16], P('dom'), may hold values from 0 to 15, each once
- ancestors: int32 [16], P('dom'), may hold values from 0 to 15, as said below
- prior_weight: float32 [16], P('dom'), may hold values from 0.01 to 1
Outputs:
- final_depth: float32 [16, 32, 256, 512], P('dom', 'space')
- final_infiltrated: float32 [16, 32, 256, 512], P('dom', 'space')
- weights: float32 [16], P('dom')
Inputs may be any that keep to these rules, and one draw needn't show every extreme that they name: `ancestors`: the ancestor of slot s is a slot of its own group, 2 * (s // 2) to 2 * (s // 2) + 1; slot 0's ancestor is 0 and the last slot's is itself.
All inputs are finite; a program needn't handle non-finite values.
Results may differ from a plain program's by a relative error of at most 0.0003.
Values may be sent and summed in bfloat16 or wider, within the bound.
No kernel may reach another device: no remote copies, remote signals or barrier semaphores. Data moves between devices by JAX's collectives and lax.ppermute only.
A program may use at most 64 MiB of HBM per device.

v0:
```python
import jax
import jax.numpy as jnp
from jax import lax
from jax.sharding import PartitionSpec as P

TX = 4
SUB = 6
HOURS = 2
time_step = 0.01
slope_floor = 0.1
sharpness = 20.0


def passed_along(block, axis, distance):
    devices = range(lax.axis_size(axis))
    route = [(i - distance, i) for i in devices if i - distance in devices]
    return lax.ppermute(block, axis, route)


def passed_along_2(array, axis, by):
    devices = lax.axis_size(axis)
    return lax.ppermute(array, axis, [(i, (i + by) % devices) for i in range(devices)])


def shift_rows(edge, offset):
    return passed_along(edge, "space", offset)


def shift_cols(edge, offset):
    return passed_along_2(edge, "space", offset)


def from_west(edge, column_tile, shifter):
    near = shifter(edge, 1)
    far = shifter(edge, -(TX - 1))
    return jnp.where(column_tile == 0, far, near)


def from_east(edge, column_tile, shifter):
    near = shifter(edge, -1)
    far = shifter(edge, TX - 1)
    return jnp.where(column_tile == TX - 1, far, near)


def with_rims(field, column_tile):
    north = shift_rows(field[..., -1, :], TX)
    south = shift_rows(field[..., 0, :], -TX)
    west = from_west(field[..., :, -1], column_tile, shift_cols)
    east = from_east(field[..., :, 0], column_tile, shift_cols)
    tall = jnp.concatenate([north[..., None, :], field, south[..., None, :]], axis=-2)
    corner = jnp.zeros(field.shape[:-2] + (1,), field.dtype)
    west_col = jnp.concatenate([corner, west, corner], axis=-1)[..., None]
    east_col = jnp.concatenate([corner, east, corner], axis=-1)[..., None]
    return jnp.concatenate([west_col, tall, east_col], axis=-1)


def face_flux(depth_a, depth_b, level_a, level_b, rough):
    slope = level_b - level_a
    mean_depth = 0.5 * (depth_a + depth_b)
    return (
        -jnp.power(mean_depth, 5.0 / 3.0) * slope / (rough * jnp.sqrt(jnp.abs(slope) + slope_floor))
    )


def flow_step(depth_now, soak_now, padded, level, net_rain, land, conduct, suction_p, rough):
    flux_cols = face_flux(
        padded[:, 1:-1, :-1], padded[:, 1:-1, 1:], level[:, 1:-1, :-1], level[:, 1:-1, 1:], rough
    )
    flux_rows = face_flux(
        padded[:, :-1, 1:-1], padded[:, 1:, 1:-1], level[:, :-1, 1:-1], level[:, 1:, 1:-1], rough
    )
    outflow = (
        flux_cols[:, :, 1:] - flux_cols[:, :, :-1] + flux_rows[:, 1:, :] - flux_rows[:, :-1, :]
    )
    ponded = jnp.maximum(depth_now - time_step * outflow + time_step * net_rain, 0.0)
    capacity = conduct * (1.0 + suction_p / soak_now)
    intake = jnp.minimum(time_step * capacity, ponded)
    return ((ponded - intake) * land, soak_now + intake * land)


def local(
    water_depth,
    infiltrated,
    terrain,
    land_mask,
    forcing,
    observed,
    conductivity,
    suction,
    manning,
    assignment,
    ancestors,
    prior_weight,
):
    per_group = water_depth.shape[0]
    first_slot = lax.axis_index("dom") * per_group
    local_slot = ancestors - first_slot
    water = jnp.take(water_depth[:, 0], local_slot, axis=0)
    soaked = jnp.take(infiltrated[:, 0], local_slot, axis=0)
    owners = jnp.take(assignment, local_slot)
    every_slot = jnp.arange(conductivity.shape[0], dtype=jnp.int32)
    picker = owners[:, None] == every_slot[None, :]

    def lookup(table):
        return jnp.sum(jnp.where(picker, table[None, :], 0.0), axis=1)[:, None, None]

    conduct = lookup(conductivity)
    suction_p = lookup(suction)
    rough = lookup(manning)
    group_mean = jnp.mean(prior_weight)
    column_tile = lax.axis_index("space") % TX
    land = land_mask[0].astype(jnp.float32)
    ground = with_rims(terrain[0], column_tile)
    window_forcing = lax.all_gather(forcing, "dom", axis=3, tiled=True)
    misfit = jnp.zeros((per_group,), jnp.float32)
    for hour in range(HOURS):
        hour_forcing = window_forcing[hour]
        net_rain = hour_forcing[0, 0].astype(jnp.float32) - hour_forcing[1, 0].astype(jnp.float32)

        def advance(index, carry):
            depth_now, soak_now = carry
            padded = with_rims(depth_now, column_tile)
            level = padded + ground[None]
            return flow_step(
                depth_now, soak_now, padded, level, net_rain, land, conduct, suction_p, rough
            )

        water, soaked = lax.fori_loop(0, SUB, advance, (water, soaked))
        gap = water - observed[hour, 0].astype(jnp.float32)
        square = gap * gap
        misfit = misfit + jnp.sum(land * square / (1.0 + square), axis=(1, 2))
    cells = HOURS * jnp.sum(land)
    summed = lax.psum((misfit, cells), "space")
    raw = group_mean * jnp.exp(-sharpness * summed[0] / summed[1])
    total = lax.psum(jnp.sum(raw), "dom")
    weights = raw / total
    return (water[:, None], soaked[:, None], weights)


def solution(mesh):
    return jax.shard_map(
        local,
        mesh=mesh,
        in_specs=(
            P("dom", "space", None, None),
            P("dom", "space", None, None),
            P("space", None, None),
            P("space", None, None),
            P(None, None, "space", "dom", None),
            P(None, "space", None, None),
            P(),
            P(),
            P(),
            P("dom"),
            P("dom"),
            P("dom"),
        ),
        out_specs=(P("dom", "space", None, None), P("dom", "space", None, None), P("dom")),
        check_vma=False,
    )
```

profile of v0, /device:TPU:0, one launch (start us, length us, event | category | flops | bytes accessed | tf_op | source)
XLA Modules:
  0.0 788.4 jit_solution(13854615685803920261)
XLA Ops:
  53.1 27.6 %all-gather.2.cloned.1.call-done = bf16[2,2,1,256,512]{4,1,2,0,3:T(2,128)(2,1)} async-done(((bf16[2,2,1,32,512]{4,1,2,0,3:T(2,128)(2,1)}), bf16[2,2,1,256,512]{4,1,2,0,3:T(2,128)(2,1)}) %all-gather.2.cloned.1.call-update) | async-done | bytes 1048592 | tf_op jit(solution)/shard_map/all_gather | solution.py:114
  87.6 284.1 %while.28 = (s32[]{:T(128)}, f32[2,256,512]{1,0,2:T(2,128)S(1)}, f32[2,256,512]{1,0,2:T(2,128)}, pred[]{:T(512)}, pred[]{:T(512)}, /*index=5*/f32[258,514]{0,1:T...) while((s32[]{:T(128)}, f32[2,256,512]{1,0,2:T(2,128)S(1)}, ...), condition=%wide.region_4.6_spmd, body=%wide.region_3.5_spmd.sunk | while | flops 12489274 | bytes 36930208 | solution.py:128
  114.2 7.3 multiply_divide_fusion.4
  121.5 8.1 %fusion.47 = f32[2,257,512]{1,0,2:T(2,128)S(1)} fusion(f32[2,256,512]{1,0,2:T(2,128)S(1)} %get-tuple-element.585, f32[2,1,512]{1,0,2:T(2,128)S(1)} %copy.141, f32[2,1,512]{1,0,2:T(2,128)S(1)} %copy-done.5, f32[2,258,514]{1,0,2:T(2,128)S(1)} %maximum_add_fusion.6, f32[2]{0:T(128)S(1)} %bitcast.100), kind=kLoop, calls=%fused_computation.10.clone.1 | loop fusion | flops 2894848 | bytes 4214792 | tf_op jit(solution)/shard_map/while/body/eval_jaxpr/div | solution.py:61
  161.4 7.3 multiply_divide_fusion.4
  168.7 8.1 %fusion.47 = f32[2,257,512]{1,0,2:T(2,128)S(1)} fusion(f32[2,256,512]{1,0,2:T(2,128)S(1)} %get-tuple-element.585, f32[2,1,512]{1,0,2:T(2,128)S(1)} %copy.141, f32[2,1,512]{1,0,2:T(2,128)S(1)} %copy-done.5, f32[2,258,514]{1,0,2:T(2,128)S(1)} %maximum_add_fusion.6, f32[2]{0:T(128)S(1)} %bitcast.100), kind=kLoop, calls=%fused_computation.10.clone.1 | loop fusion | flops 2894848 | bytes 4214792 | tf_op jit(solution)/shard_map/while/body/eval_jaxpr/div | solution.py:61
  208.6 7.3 multiply_divide_fusion.4
  215.9 8.1 %fusion.47 = f32[2,257,512]{1,0,2:T(2,128)S(1)} fusion(f32[2,256,512]{1,0,2:T(2,128)S(1)} %get-tuple-element.585, f32[2,1,512]{1,0,2:T(2,128)S(1)} %copy.141, f32[2,1,512]{1,0,2:T(2,128)S(1)} %copy-done.5, f32[2,258,514]{1,0,2:T(2,128)S(1)} %maximum_add_fusion.6, f32[2]{0:T(128)S(1)} %bitcast.100), kind=kLoop, calls=%fused_computation.10.clone.1 | loop fusion | flops 2894848 | bytes 4214792 | tf_op jit(solution)/shard_map/while/body/eval_jaxpr/div | solution.py:61
  255.8 7.3 multiply_divide_fusion.4
  263.1 8.1 %fusion.47 = f32[2,257,512]{1,0,2:T(2,128)S(1)} fusion(f32[2,256,512]{1,0,2:T(2,128)S(1)} %get-tuple-element.585, f32[2,1,512]{1,0,2:T(2,128)S(1)} %copy.141, f32[2,1,512]{1,0,2:T(2,128)S(1)} %copy-done.5, f32[2,258,514]{1,0,2:T(2,128)S(1)} %maximum_add_fusion.6, f32[2]{0:T(128)S(1)} %bitcast.100), kind=kLoop, calls=%fused_computation.10.clone.1 | loop fusion | flops 2894848 | bytes 4214792 | tf_op jit(solution)/shard_map/while/body/eval_jaxpr/div | solution.py:61
  303.0 7.3 multiply_divide_fusion.4
  310.3 8.1 %fusion.47 = f32[2,257,512]{1,0,2:T(2,128)S(1)} fusion(f32[2,256,512]{1,0,2:T(2,128)S(1)} %get-tuple-element.585, f32[2,1,512]{1,0,2:T(2,128)S(1)} %copy.141, f32[2,1,512]{1,0,2:T(2,128)S(1)} %copy-done.5, f32[2,258,514]{1,0,2:T(2,128)S(1)} %maximum_add_fusion.6, f32[2]{0:T(128)S(1)} %bitcast.100), kind=kLoop, calls=%fused_computation.10.clone.1 | loop fusion | flops 2894848 | bytes 4214792 | tf_op jit(solution)/shard_map/while/body/eval_jaxpr/div | solution.py:61
  323.9 6.9 collective-permute-start.2
  350.6 7.3 multiply_divide_fusion.4
  357.9 8.1 %fusion.47 = f32[2,257,512]{1,0,2:T(2,128)S(1)} fusion(f32[2,256,512]{1,0,2:T(2,128)S(1)} %get-tuple-element.585, f32[2,1,512]{1,0,2:T(2,128)S(1)} %copy.141, f32[2,1,512]{1,0,2:T(2,128)S(1)} %copy-done.5, f32[2,258,514]{1,0,2:T(2,128)S(1)} %maximum_add_fusion.6, f32[2]{0:T(128)S(1)} %bitcast.100), kind=kLoop, calls=%fused_computation.10.clone.1 | loop fusion | flops 2894848 | bytes 4214792 | tf_op jit(solution)/shard_map/while/body/eval_jaxpr/div | solution.py:61
  372.9 298.5 %while.29 = (s32[]{:T(128)}, f32[2,256,512]{1,0,2:T(2,128)S(1)}, f32[2,256,512]{1,0,2:T(2,128)}, pred[]{:T(512)}, pred[]{:T(512)}, /*index=5*/f32[258,514]{0,1:T...) while((s32[]{:T(128)}, f32[2,256,512]{1,0,2:T(2,128)S(1)}, ...), condition=%wide.region_6.8_spmd, body=%wide.region_5.7_spmd.sunk | while | flops 12489274 | bytes 39043804 | solution.py:128
  373.0 7.5 collective-permute-start.8
  402.3 7.3 multiply_divide_fusion.5
  409.6 8.1 %fusion.50 = f32[2,257,512]{1,0,2:T(2,128)S(1)} fusion(f32[2,256,512]{1,0,2:T(2,128)S(1)} %get-tuple-element.624, f32[2,1,512]{1,0,2:T(2,128)S(1)} %copy-done.4, f32[2,1,512]{1,0,2:T(2,128)S(1)} %copy-done.6, f32[2,258,514]{1,0,2:T(2,128)S(1)} %maximum_add_fusion.7, f32[2]{0:T(128)S(1)} %bitcast.102), kind=kLoop, calls=%fused_computation.50.clone.1 | loop fusion | flops 2894848 | bytes 4214792 | tf_op jit(solution)/shard_map/while/body/eval_jaxpr/div | solution.py:61
  423.3 7.2 collective-permute-start.8
  452.3 7.3 multiply_divide_fusion.5
  459.6 8.1 %fusion.50 = f32[2,257,512]{1,0,2:T(2,128)S(1)} fusion(f32[2,256,512]{1,0,2:T(2,128)S(1)} %get-tuple-element.624, f32[2,1,512]{1,0,2:T(2,128)S(1)} %copy-done.4, f32[2,1,512]{1,0,2:T(2,128)S(1)} %copy-done.6, f32[2,258,514]{1,0,2:T(2,128)S(1)} %maximum_add_fusion.7, f32[2]{0:T(128)S(1)} %bitcast.102), kind=kLoop, calls=%fused_computation.50.clone.1 | loop fusion | flops 2894848 | bytes 4214792 | tf_op jit(solution)/shard_map/while/body/eval_jaxpr/div | solution.py:61
  501.8 7.3 multiply_divide_fusion.5
  509.1 8.1 %fusion.50 = f32[2,257,512]{1,0,2:T(2,128)S(1)} fusion(f32[2,256,512]{1,0,2:T(2,128)S(1)} %get-tuple-element.624, f32[2,1,512]{1,0,2:T(2,128)S(1)} %copy-done.4, f32[2,1,512]{1,0,2:T(2,128)S(1)} %copy-done.6, f32[2,258,514]{1,0,2:T(2,128)S(1)} %maximum_add_fusion.7, f32[2]{0:T(128)S(1)} %bitcast.102), kind=kLoop, calls=%fused_computation.50.clone.1 | loop fusion | flops 2894848 | bytes 4214792 | tf_op jit(solution)/shard_map/while/body/eval_jaxpr/div | solution.py:61
  551.4 7.3 multiply_divide_fusion.5
  558.7 8.1 %fusion.50 = f32[2,257,512]{1,0,2:T(2,128)S(1)} fusion(f32[2,256,512]{1,0,2:T(2,128)S(1)} %get-tuple-element.624, f32[2,1,512]{1,0,2:T(2,128)S(1)} %copy-done.4, f32[2,1,512]{1,0,2:T(2,128)S(1)} %copy-done.6, f32[2,258,514]{1,0,2:T(2,128)S(1)} %maximum_add_fusion.7, f32[2]{0:T(128)S(1)} %bitcast.102), kind=kLoop, calls=%fused_computation.50.clone.1 | loop fusion | flops 2894848 | bytes 4214792 | tf_op jit(solution)/shard_map/while/body/eval_jaxpr/div | solution.py:61
  600.9 7.3 multiply_divide_fusion.5
  608.2 8.1 %fusion.50 = f32[2,257,512]{1,0,2:T(2,128)S(1)} fusion(f32[2,256,512]{1,0,2:T(2,128)S(1)} %get-tuple-element.624, f32[2,1,512]{1,0,2:T(2,128)S(1)} %copy-done.4, f32[2,1,512]{1,0,2:T(2,128)S(1)} %copy-done.6, f32[2,258,514]{1,0,2:T(2,128)S(1)} %maximum_add_fusion.7, f32[2]{0:T(128)S(1)} %bitcast.102), kind=kLoop, calls=%fused_computation.50.clone.1 | loop fusion | flops 2894848 | bytes 4214792 | tf_op jit(solution)/shard_map/while/body/eval_jaxpr/div | solution.py:61
  650.5 7.3 multiply_divide_fusion.5
  657.8 8.1 %fusion.50 = f32[2,257,512]{1,0,2:T(2,128)S(1)} fusion(f32[2,256,512]{1,0,2:T(2,128)S(1)} %get-tuple-element.624, f32[2,1,512]{1,0,2:T(2,128)S(1)} %copy-done.4, f32[2,1,512]{1,0,2:T(2,128)S(1)} %copy-done.6, f32[2,258,514]{1,0,2:T(2,128)S(1)} %maximum_add_fusion.7, f32[2]{0:T(128)S(1)} %bitcast.102), kind=kLoop, calls=%fused_computation.50.clone.1 | loop fusion | flops 2894848 | bytes 4214792 | tf_op jit(solution)/shard_map/while/body/eval_jaxpr/div | solution.py:61
  678.7 72.3 %all-reduce = (f32[2]{0:T(128)S(1)}, f32[]{:T(128)}) all-reduce(f32[2]{0:T(128)S(1)} %add.160, f32[]{:T(128)S(6)} %mul.249), channel_id=1, replica_groups=mesh['space'=32,'dom'=8] {'space'}, use_global_device_ids=true, to_apply=%region_10.12 | all-reduce | flops 3 | bytes 24 | tf_op jit(solution)/shard_map/psum | solution.py:133
  752.4 27.7 %psum.23 = f32[]{:T(128)} all-reduce(f32[]{:T(128)} %get-tuple-element.375), channel_id=1, replica_groups=mesh['space'=32,'dom'=8] {'dom'}, use_global_device_ids=true, to_apply=%region_14.16 | all-reduce | flops 1 | bytes 8 | tf_op jit(solution)/shard_map/psum | solution.py:135
  (503 shorter events, 436.2 us)
Async XLA Ops:
  7.2 73.5 %all-gather.2.cloned.1.call-start = ((), (), s32[]{:S(2)}) async-start(), calls=%async_computation | async-start | bytes 1179648 | tf_op jit(solution)/shard_map/all_gather | solution.py:114
  8.6 33.9 %collective-permute-start.17 = (f32[256]{0:T(256)S(1)}, f32[256]{0:T(256)S(1)}, u32[]{:S(2)}, u32[]{:S(2)}) collective-permute-start(f32[256]{0:T(256)S(1)} %bitcast.123), channel_id=1, source_target_pairs={{0,248},{8,0},{16,8},{24,16},{32,24},{40,32},{48,40},{56,48},{64,5... | collective-permute-start | bytes 3080 | tf_op jit(solution)/shard_map/ppermute | solution.py:22
  13.5 35.1 %collective-permute-start.16 = (f32[256]{0:T(256)S(1)}, f32[256]{0:T(256)S(1)}, u32[]{:S(2)}, u32[]{:S(2)}) collective-permute-start(f32[256]{0:T(256)S(1)} %bitcast.124), channel_id=1, source_target_pairs={{0,24},{8,32},{16,40},{24,48},{32,56},{40,64},{48,72},{56,80},{64,... | collective-permute-start | bytes 3080 | tf_op jit(solution)/shard_map/ppermute | solution.py:22
  13.5 35.2 %collective-permute-start.13 = (f32[256]{0:T(256)S(1)}, f32[256]{0:T(256)S(1)}, u32[]{:S(2)}, u32[]{:S(2)}) collective-permute-start(f32[256]{0:T(256)S(1)} %bitcast.121), channel_id=1, source_target_pairs={{0,8},{8,16},{16,24},{24,32},{32,40},{40,48},{48,56},{56,64},{64,7... | collective-permute-start | bytes 3080 | tf_op jit(solution)/shard_map/ppermute | solution.py:22
  13.5 35.2 %collective-permute-start.12 = (f32[256]{0:T(256)S(1)}, f32[256]{0:T(256)S(1)}, u32[]{:S(2)}, u32[]{:S(2)}) collective-permute-start(f32[256]{0:T(256)S(1)} %bitcast.122), channel_id=1, source_target_pairs={{0,232},{8,240},{16,248},{24,0},{32,8},{40,16},{48,24},{56,32},{64... | collective-permute-start | bytes 3080 | tf_op jit(solution)/shard_map/ppermute | solution.py:22
  87.9 18.8 %collective-permute-start.2 = (f32[2,256]{1,0:T(2,128)S(1)}, f32[2,256]{1,0:T(2,128)S(1)}, u32[]{:S(2)}, u32[]{:S(2)}) collective-permute-start(f32[2,256]{1,0:T(2,128)S(1)} %get-tuple-element.544), channel_id=1, source_target_pairs={{0,232},{8,240},{16,248},{24,0},{32,8},{40,16},{48,24},{56,32},{64... | collective-permute-start | bytes 6152 | tf_op jit(solution)/shard_map/while/body/eval_jaxpr/ppermute | solution.py:22
  91.1 15.7 %collective-permute-start.5 = (f32[2,256]{1,0:T(2,128)S(1)}, f32[2,256]{1,0:T(2,128)S(1)}, u32[]{:S(2)}, u32[]{:S(2)}) collective-permute-start(f32[2,256]{1,0:T(2,128)S(1)} %get-tuple-element.545), channel_id=1, source_target_pairs={{0,248},{8,0},{16,8},{24,16},{32,24},{40,32},{48,40},{56,48},{64,5... | collective-permute-start | bytes 6152 | tf_op jit(solution)/shard_map/while/body/eval_jaxpr/ppermute | solution.py:22
  135.1 18.8 %collective-permute-start.2 = (f32[2,256]{1,0:T(2,128)S(1)}, f32[2,256]{1,0:T(2,128)S(1)}, u32[]{:S(2)}, u32[]{:S(2)}) collective-permute-start(f32[2,256]{1,0:T(2,128)S(1)} %get-tuple-element.544), channel_id=1, source_target_pairs={{0,232},{8,240},{16,248},{24,0},{32,8},{40,16},{48,24},{56,32},{64... | collective-permute-start | bytes 6152 | tf_op jit(solution)/shard_map/while/body/eval_jaxpr/ppermute | solution.py:22
  138.9 15.1 %collective-permute-start.5 = (f32[2,256]{1,0:T(2,128)S(1)}, f32[2,256]{1,0:T(2,128)S(1)}, u32[]{:S(2)}, u32[]{:S(2)}) collective-permute-start(f32[2,256]{1,0:T(2,128)S(1)} %get-tuple-element.545), channel_id=1, source_target_pairs={{0,248},{8,0},{16,8},{24,16},{32,24},{40,32},{48,40},{56,48},{64,5... | collective-permute-start | bytes 6152 | tf_op jit(solution)/shard_map/while/body/eval_jaxpr/ppermute | solution.py:22
  182.3 18.8 %collective-permute-start.2 = (f32[2,256]{1,0:T(2,128)S(1)}, f32[2,256]{1,0:T(2,128)S(1)}, u32[]{:S(2)}, u32[]{:S(2)}) collective-permute-start(f32[2,256]{1,0:T(2,128)S(1)} %get-tuple-element.544), channel_id=1, source_target_pairs={{0,232},{8,240},{16,248},{24,0},{32,8},{40,16},{48,24},{56,32},{64... | collective-permute-start | bytes 6152 | tf_op jit(solution)/shard_map/while/body/eval_jaxpr/ppermute | solution.py:22
  187.5 13.7 %collective-permute-start.5 = (f32[2,256]{1,0:T(2,128)S(1)}, f32[2,256]{1,0:T(2,128)S(1)}, u32[]{:S(2)}, u32[]{:S(2)}) collective-permute-start(f32[2,256]{1,0:T(2,128)S(1)} %get-tuple-element.545), channel_id=1, source_target_pairs={{0,248},{8,0},{16,8},{24,16},{32,24},{40,32},{48,40},{56,48},{64,5... | collective-permute-start | bytes 6152 | tf_op jit(solution)/shard_map/while/body/eval_jaxpr/ppermute | solution.py:22
  229.5 18.8 %collective-permute-start.2 = (f32[2,256]{1,0:T(2,128)S(1)}, f32[2,256]{1,0:T(2,128)S(1)}, u32[]{:S(2)}, u32[]{:S(2)}) collective-permute-start(f32[2,256]{1,0:T(2,128)S(1)} %get-tuple-element.544), channel_id=1, source_target_pairs={{0,232},{8,240},{16,248},{24,0},{32,8},{40,16},{48,24},{56,32},{64... | collective-permute-start | bytes 6152 | tf_op jit(solution)/shard_map/while/body/eval_jaxpr/ppermute | solution.py:22
  234.9 13.5 %collective-permute-start.5 = (f32[2,256]{1,0:T(2,128)S(1)}, f32[2,256]{1,0:T(2,128)S(1)}, u32[]{:S(2)}, u32[]{:S(2)}) collective-permute-start(f32[2,256]{1,0:T(2,128)S(1)} %get-tuple-element.545), channel_id=1, source_target_pairs={{0,248},{8,0},{16,8},{24,16},{32,24},{40,32},{48,40},{56,48},{64,5... | collective-permute-start | bytes 6152 | tf_op jit(solution)/shard_map/while/body/eval_jaxpr/ppermute | solution.py:22
  276.7 18.9 %collective-permute-start.2 = (f32[2,256]{1,0:T(2,128)S(1)}, f32[2,256]{1,0:T(2,128)S(1)}, u32[]{:S(2)}, u32[]{:S(2)}) collective-permute-start(f32[2,256]{1,0:T(2,128)S(1)} %get-tuple-element.544), channel_id=1, source_target_pairs={{0,232},{8,240},{16,248},{24,0},{32,8},{40,16},{48,24},{56,32},{64... | collective-permute-start | bytes 6152 | tf_op jit(solution)/shard_map/while/body/eval_jaxpr/ppermute | solution.py:22
  323.9 19.2 %collective-permute-start.2 = (f32[2,256]{1,0:T(2,128)S(1)}, f32[2,256]{1,0:T(2,128)S(1)}, u32[]{:S(2)}, u32[]{:S(2)}) collective-permute-start(f32[2,256]{1,0:T(2,128)S(1)} %get-tuple-element.544), channel_id=1, source_target_pairs={{0,232},{8,240},{16,248},{24,0},{32,8},{40,16},{48,24},{56,32},{64... | collective-permute-start | bytes 6152 | tf_op jit(solution)/shard_map/while/body/eval_jaxpr/ppermute | solution.py:22
  372.9 15.0 %collective-permute-start.9 = (f32[2,256]{1,0:T(2,128)S(1)}, f32[2,256]{1,0:T(2,128)S(1)}, u32[]{:S(2)}, u32[]{:S(2)}) collective-permute-start(f32[2,256]{1,0:T(2,128)S(1)} %get-tuple-element.564), channel_id=1, source_target_pairs={{0,8},{8,16},{16,24},{24,32},{32,40},{40,48},{48,56},{56,64},{64,7... | collective-permute-start | bytes 6152 | tf_op jit(solution)/shard_map/while/body/eval_jaxpr/ppermute | solution.py:22
  373.0 20.9 %collective-permute-start.8 = (f32[2,256]{1,0:T(2,128)S(1)}, f32[2,256]{1,0:T(2,128)S(1)}, u32[]{:S(2)}, u32[]{:S(2)}) collective-permute-start(f32[2,256]{1,0:T(2,128)S(1)} %get-tuple-element.564), channel_id=1, source_target_pairs={{0,232},{8,240},{16,248},{24,0},{32,8},{40,16},{48,24},{56,32},{64... | collective-permute-start | bytes 6152 | tf_op jit(solution)/shard_map/while/body/eval_jaxpr/ppermute | solution.py:22
  380.5 13.5 %collective-permute-start.11 = (f32[2,256]{1,0:T(2,128)S(1)}, f32[2,256]{1,0:T(2,128)S(1)}, u32[]{:S(2)}, u32[]{:S(2)}) collective-permute-start(f32[2,256]{1,0:T(2,128)S(1)} %get-tuple-element.565), channel_id=1, source_target_pairs={{0,248},{8,0},{16,8},{24,16},{32,24},{40,32},{48,40},{56,48},{64,5... | collective-permute-start | bytes 6152 | tf_op jit(solution)/shard_map/while/body/eval_jaxpr/ppermute | solution.py:22
  423.3 14.6 %collective-permute-start.9 = (f32[2,256]{1,0:T(2,128)S(1)}, f32[2,256]{1,0:T(2,128)S(1)}, u32[]{:S(2)}, u32[]{:S(2)}) collective-permute-start(f32[2,256]{1,0:T(2,128)S(1)} %get-tuple-element.564), channel_id=1, source_target_pairs={{0,8},{8,16},{16,24},{24,32},{32,40},{40,48},{48,56},{56,64},{64,7... | collective-permute-start | bytes 6152 | tf_op jit(solution)/shard_map/while/body/eval_jaxpr/ppermute | solution.py:22
  423.3 20.7 %collective-permute-start.8 = (f32[2,256]{1,0:T(2,128)S(1)}, f32[2,256]{1,0:T(2,128)S(1)}, u32[]{:S(2)}, u32[]{:S(2)}) collective-permute-start(f32[2,256]{1,0:T(2,128)S(1)} %get-tuple-element.564), channel_id=1, source_target_pairs={{0,232},{8,240},{16,248},{24,0},{32,8},{40,16},{48,24},{56,32},{64... | collective-permute-start | bytes 6152 | tf_op jit(solution)/shard_map/while/body/eval_jaxpr/ppermute | solution.py:22
  430.5 13.5 %collective-permute-start.11 = (f32[2,256]{1,0:T(2,128)S(1)}, f32[2,256]{1,0:T(2,128)S(1)}, u32[]{:S(2)}, u32[]{:S(2)}) collective-permute-start(f32[2,256]{1,0:T(2,128)S(1)} %get-tuple-element.565), channel_id=1, source_target_pairs={{0,248},{8,0},{16,8},{24,16},{32,24},{40,32},{48,40},{56,48},{64,5... | collective-permute-start | bytes 6152 | tf_op jit(solution)/shard_map/while/body/eval_jaxpr/ppermute | solution.py:22
  473.3 14.1 %collective-permute-start.9 = (f32[2,256]{1,0:T(2,128)S(1)}, f32[2,256]{1,0:T(2,128)S(1)}, u32[]{:S(2)}, u32[]{:S(2)}) collective-permute-start(f32[2,256]{1,0:T(2,128)S(1)} %get-tuple-element.564), channel_id=1, source_target_pairs={{0,8},{8,16},{16,24},{24,32},{32,40},{40,48},{48,56},{56,64},{64,7... | collective-permute-start | bytes 6152 | tf_op jit(solution)/shard_map/while/body/eval_jaxpr/ppermute | solution.py:22
  473.3 20.2 %collective-permute-start.8 = (f32[2,256]{1,0:T(2,128)S(1)}, f32[2,256]{1,0:T(2,128)S(1)}, u32[]{:S(2)}, u32[]{:S(2)}) collective-permute-start(f32[2,256]{1,0:T(2,128)S(1)} %get-tuple-element.564), channel_id=1, source_target_pairs={{0,232},{8,240},{16,248},{24,0},{32,8},{40,16},{48,24},{56,32},{64... | collective-permute-start | bytes 6152 | tf_op jit(solution)/shard_map/while/body/eval_jaxpr/ppermute | solution.py:22
  480.1 13.4 %collective-permute-start.10 = (f32[2,256]{1,0:T(2,128)S(1)}, f32[2,256]{1,0:T(2,128)S(1)}, u32[]{:S(2)}, u32[]{:S(2)}) collective-permute-start(f32[2,256]{1,0:T(2,128)S(1)} %get-tuple-element.565), channel_id=1, source_target_pairs={{0,24},{8,32},{16,40},{24,48},{32,56},{40,64},{48,72},{56,80},{64,... | collective-permute-start | bytes 6152 | tf_op jit(solution)/shard_map/while/body/eval_jaxpr/ppermute | solution.py:22
  522.8 14.2 %collective-permute-start.9 = (f32[2,256]{1,0:T(2,128)S(1)}, f32[2,256]{1,0:T(2,128)S(1)}, u32[]{:S(2)}, u32[]{:S(2)}) collective-permute-start(f32[2,256]{1,0:T(2,128)S(1)} %get-tuple-element.564), channel_id=1, source_target_pairs={{0,8},{8,16},{16,24},{24,32},{32,40},{40,48},{48,56},{56,64},{64,7... | collective-permute-start | bytes 6152 | tf_op jit(solution)/shard_map/while/body/eval_jaxpr/ppermute | solution.py:22
  522.8 20.2 %collective-permute-start.8 = (f32[2,256]{1,0:T(2,128)S(1)}, f32[2,256]{1,0:T(2,128)S(1)}, u32[]{:S(2)}, u32[]{:S(2)}) collective-permute-start(f32[2,256]{1,0:T(2,128)S(1)} %get-tuple-element.564), channel_id=1, source_target_pairs={{0,232},{8,240},{16,248},{24,0},{32,8},{40,16},{48,24},{56,32},{64... | collective-permute-start | bytes 6152 | tf_op jit(solution)/shard_map/while/body/eval_jaxpr/ppermute | solution.py:22
  529.6 13.4 %collective-permute-start.10 = (f32[2,256]{1,0:T(2,128)S(1)}, f32[2,256]{1,0:T(2,128)S(1)}, u32[]{:S(2)}, u32[]{:S(2)}) collective-permute-start(f32[2,256]{1,0:T(2,128)S(1)} %get-tuple-element.565), channel_id=1, source_target_pairs={{0,24},{8,32},{16,40},{24,48},{32,56},{40,64},{48,72},{56,80},{64,... | collective-permute-start | bytes 6152 | tf_op jit(solution)/shard_map/while/body/eval_jaxpr/ppermute | solution.py:22
  572.3 14.2 %collective-permute-start.9 = (f32[2,256]{1,0:T(2,128)S(1)}, f32[2,256]{1,0:T(2,128)S(1)}, u32[]{:S(2)}, u32[]{:S(2)}) collective-permute-start(f32[2,256]{1,0:T(2,128)S(1)} %get-tuple-element.564), channel_id=1, source_target_pairs={{0,8},{8,16},{16,24},{24,32},{32,40},{40,48},{48,56},{56,64},{64,7... | collective-permute-start | bytes 6152 | tf_op jit(solution)/shard_map/while/body/eval_jaxpr/ppermute | solution.py:22
  572.3 20.2 %collective-permute-start.8 = (f32[2,256]{1,0:T(2,128)S(1)}, f32[2,256]{1,0:T(2,128)S(1)}, u32[]{:S(2)}, u32[]{:S(2)}) collective-permute-start(f32[2,256]{1,0:T(2,128)S(1)} %get-tuple-element.564), channel_id=1, source_target_pairs={{0,232},{8,240},{16,248},{24,0},{32,8},{40,16},{48,24},{56,32},{64... | collective-permute-start | bytes 6152 | tf_op jit(solution)/shard_map/while/body/eval_jaxpr/ppermute | solution.py:22
  579.2 13.4 %collective-permute-start.10 = (f32[2,256]{1,0:T(2,128)S(1)}, f32[2,256]{1,0:T(2,128)S(1)}, u32[]{:S(2)}, u32[]{:S(2)}) collective-permute-start(f32[2,256]{1,0:T(2,128)S(1)} %get-tuple-element.565), channel_id=1, source_target_pairs={{0,24},{8,32},{16,40},{24,48},{32,56},{40,64},{48,72},{56,80},{64,... | collective-permute-start | bytes 6152 | tf_op jit(solution)/shard_map/while/body/eval_jaxpr/ppermute | solution.py:22
  621.9 14.2 %collective-permute-start.9 = (f32[2,256]{1,0:T(2,128)S(1)}, f32[2,256]{1,0:T(2,128)S(1)}, u32[]{:S(2)}, u32[]{:S(2)}) collective-permute-start(f32[2,256]{1,0:T(2,128)S(1)} %get-tuple-element.564), channel_id=1, source_target_pairs={{0,8},{8,16},{16,24},{24,32},{32,40},{40,48},{48,56},{56,64},{64,7... | collective-permute-start | bytes 6152 | tf_op jit(solution)/shard_map/while/body/eval_jaxpr/ppermute | solution.py:22
  621.9 20.2 %collective-permute-start.8 = (f32[2,256]{1,0:T(2,128)S(1)}, f32[2,256]{1,0:T(2,128)S(1)}, u32[]{:S(2)}, u32[]{:S(2)}) collective-permute-start(f32[2,256]{1,0:T(2,128)S(1)} %get-tuple-element.564), channel_id=1, source_target_pairs={{0,232},{8,240},{16,248},{24,0},{32,8},{40,16},{48,24},{56,32},{64... | collective-permute-start | bytes 6152 | tf_op jit(solution)/shard_map/while/body/eval_jaxpr/ppermute | solution.py:22
  (117 other events, 927.4 us)
Sparse Core Ops, SparseCore 0:
  21.3 59.3 all-gather.1
where the time goes:
time: 797 us; the launch traced here: 788 us
  other arithmetic  349 us (44%)
  starting transfers between devices  189 us (24%)
  blocking collectives  100 us (13%)
  local copies, waits for them, and re-layouts  89.5 us (11%)
  waiting for transfers between devices  42.8 us (5%)
  between operations  15.9 us (2%)
    div x24, other arithmetic, face_flux(): -jnp.power(mean_depth, 5.0 / 3.0) * slope  185 us
    ppermute x26, starting transfers between devices, passed_along(): return lax.ppermute(block, axis, route)  95.5 us
    ppermute x52, starting transfers between devices, passed_along_2(): lax.ppermute(array, axis, [(i, (i + by) % devices) for i in range(devices)])  93.4 us
    psum x1, blocking collectives, local(): summed = lax.psum((misfit, cells), 'space')  72.3 us
    add x12, other arithmetic, advance(): level = padded + ground[None]  58.6 us
    add x12, other arithmetic, flow_step(): return ((ponded - intake) * land, soak_now + intake * land)  53.9 us
    slice x24, local copies, waits for them, and re-layouts, with_rims(): south = shift_rows(field[..., 0, :], -TX)  33.9 us
    psum x1, blocking collectives, local(): total = lax.psum(jnp.sum(raw), 'dom')  27.7 us
  transfers between devices with their start and end apart: 79, of which 14 were waited for; matrix products, arithmetic and copies ran while one was open for 12% of the time, Pallas kernels for 0%

commit v1 on v0

--- a/solution.py
+++ b/solution.py
@@ -111,7 +111,9 @@
     column_tile = lax.axis_index("space") % TX
     land = land_mask[0].astype(jnp.float32)
     ground = with_rims(terrain[0], column_tile)
-    window_forcing = lax.all_gather(forcing, "dom", axis=3, tiled=True)
+    window_forcing = jnp.concatenate(
+        lax.all_to_all(jnp.stack([forcing] * lax.axis_size("dom")), "dom", 0, 0), axis=3
+    )
     misfit = jnp.zeros((per_group,), jnp.float32)
     for hour in range(HOURS):
         hour_forcing = window_forcing[hour]

time: 797 us -> 768 us (0.964)
  waiting for transfers between devices: 42.8 us -> 15.3 us
  between operations: 15.9 us -> 2.44 us
  starting transfers between devices: 189 us -> 198 us
    all_gather x1 -> x0, waiting for transfers between devices: 27.6 us -> none  [local(): window_forcing = lax.all_gather(forcing, 'dom', axis=3, tiled=True)]
    all_to_all x0 -> x1, starting transfers between devices: none -> 8.36 us  [local(): lax.all_to_all(jnp.stack([forcing] * lax.axis_size('dom')), 'dom', 0, 0)]
  transfers between devices with their start and end apart: 79 -> 79, of which waited for: 14 -> 13; matrix products, arithmetic and copies ran while one was open for 12% -> 13% of each run, Pallas kernels for 0% -> 0%
where the time goes in v1:
time: 768 us; the launch traced here: 760 us
  other arithmetic  344 us (45%)
  starting transfers between devices  198 us (26%)
  blocking collectives  105 us (14%)
  local copies, waits for them, and re-layouts  92.7 us (12%)
  waiting for transfers between devices  15.3 us (2%)
    div x24, other arithmetic, face_flux(): -jnp.power(mean_depth, 5.0 / 3.0) * slope  185 us
    ppermute x26, starting transfers between devices, passed_along(): return lax.ppermute(block, axis, route)  95.5 us
    ppermute x52, starting transfers between devices, passed_along_2(): lax.ppermute(array, axis, [(i, (i + by) % devices) for i in range(devices)])  93.8 us
    psum x1, blocking collectives, local(): summed = lax.psum((misfit, cells), 'space')  72.8 us
    add x12, other arithmetic, advance(): level = padded + ground[None]  58.6 us
    add x12, other arithmetic, flow_step(): return ((ponded - intake) * land, soak_now + intake * land)  53.9 us
    slice x24, local copies, waits for them, and re-layouts, with_rims(): south = shift_rows(field[..., 0, :], -TX)  33.9 us
    psum x1, blocking collectives, local(): total = lax.psum(jnp.sum(raw), 'dom')  32.4 us
  transfers between devices with their start and end apart: 79, of which 13 were waited for; matrix products, arithmetic and copies ran while one was open for 13% of the time, Pallas kernels for 0%

profile of v1, /device:TPU:0, one launch (start us, length us, event | category | flops | bytes accessed | tf_op | source)
XLA Modules:
  0.0 759.8 jit_solution(466662421134141013)
XLA Ops:
  14.8 8.4 %all-to-all-start = ((bf16[8,2,2,1,32,512]{5,4,3,2,1,0:T(8,128)(2,1)}), bf16[8,2,2,1,32,512]{5,4,3,2,1,0:T(8,128)(2,1)}, u32[]{:S(2)}, u32[]{:S(2)}) async-start(bf16[8,2,2,1,32,512]{5,4,3,2,1,0:T(8,128)(2,1)} %stack.2), calls=%async_computation | async-start | bytes 2097152 | tf_op jit(solution)/shard_map/all_to_all | solution.py:115
  60.0 285.0 %while.28 = (s32[]{:T(128)}, f32[2,256,512]{1,0,2:T(2,128)S(1)}, f32[2,256,512]{1,0,2:T(2,128)}, pred[]{:T(512)}, pred[]{:T(512)}, /*index=5*/f32[258,514]{0,1:T...) while((s32[]{:T(128)}, f32[2,256,512]{1,0,2:T(2,128)S(1)}, ...), condition=%wide.region_4.6_spmd, body=%wide.region_3.5_spmd.sunk | while | flops 12489274 | bytes 36930208 | solution.py:130
  86.5 7.3 multiply_divide_fusion.4
  93.8 8.1 %fusion.45 = f32[2,257,512]{1,0,2:T(2,128)S(1)} fusion(f32[2,256,512]{1,0,2:T(2,128)S(1)} %get-tuple-element.607, f32[2,1,512]{1,0,2:T(2,128)S(1)} %copy.143, f32[2,1,512]{1,0,2:T(2,128)S(1)} %copy-done.5, f32[2,258,514]{1,0,2:T(2,128)S(1)} %maximum_add_fusion.6, f32[2]{0:T(128)S(1)} %bitcast.105), kind=kLoop, calls=%fused_computation.10.clone.1 | loop fusion | flops 2894848 | bytes 4214792 | tf_op jit(solution)/shard_map/while/body/eval_jaxpr/div | solution.py:61
  133.8 7.3 multiply_divide_fusion.4
  141.0 8.1 %fusion.45 = f32[2,257,512]{1,0,2:T(2,128)S(1)} fusion(f32[2,256,512]{1,0,2:T(2,128)S(1)} %get-tuple-element.607, f32[2,1,512]{1,0,2:T(2,128)S(1)} %copy.143, f32[2,1,512]{1,0,2:T(2,128)S(1)} %copy-done.5, f32[2,258,514]{1,0,2:T(2,128)S(1)} %maximum_add_fusion.6, f32[2]{0:T(128)S(1)} %bitcast.105), kind=kLoop, calls=%fused_computation.10.clone.1 | loop fusion | flops 2894848 | bytes 4214792 | tf_op jit(solution)/shard_map/while/body/eval_jaxpr/div | solution.py:61
  181.0 7.3 multiply_divide_fusion.4
  188.3 8.1 %fusion.45 = f32[2,257,512]{1,0,2:T(2,128)S(1)} fusion(f32[2,256,512]{1,0,2:T(2,128)S(1)} %get-tuple-element.607, f32[2,1,512]{1,0,2:T(2,128)S(1)} %copy.143, f32[2,1,512]{1,0,2:T(2,128)S(1)} %copy-done.5, f32[2,258,514]{1,0,2:T(2,128)S(1)} %maximum_add_fusion.6, f32[2]{0:T(128)S(1)} %bitcast.105), kind=kLoop, calls=%fused_computation.10.clone.1 | loop fusion | flops 2894848 | bytes 4214792 | tf_op jit(solution)/shard_map/while/body/eval_jaxpr/div | solution.py:61
  228.2 7.3 multiply_divide_fusion.4
  235.5 8.1 %fusion.45 = f32[2,257,512]{1,0,2:T(2,128)S(1)} fusion(f32[2,256,512]{1,0,2:T(2,128)S(1)} %get-tuple-element.607, f32[2,1,512]{1,0,2:T(2,128)S(1)} %copy.143, f32[2,1,512]{1,0,2:T(2,128)S(1)} %copy-done.5, f32[2,258,514]{1,0,2:T(2,128)S(1)} %maximum_add_fusion.6, f32[2]{0:T(128)S(1)} %bitcast.105), kind=kLoop, calls=%fused_computation.10.clone.1 | loop fusion | flops 2894848 | bytes 4214792 | tf_op jit(solution)/shard_map/while/body/eval_jaxpr/div | solution.py:61
  275.5 7.3 multiply_divide_fusion.4
  282.7 8.1 %fusion.45 = f32[2,257,512]{1,0,2:T(2,128)S(1)} fusion(f32[2,256,512]{1,0,2:T(2,128)S(1)} %get-tuple-element.607, f32[2,1,512]{1,0,2:T(2,128)S(1)} %copy.143, f32[2,1,512]{1,0,2:T(2,128)S(1)} %copy-done.5, f32[2,258,514]{1,0,2:T(2,128)S(1)} %maximum_add_fusion.6, f32[2]{0:T(128)S(1)} %bitcast.105), kind=kLoop, calls=%fused_computation.10.clone.1 | loop fusion | flops 2894848 | bytes 4214792 | tf_op jit(solution)/shard_map/while/body/eval_jaxpr/div | solution.py:61
  296.4 7.8 %collective-permute-start.2 = (f32[2,256]{1,0:T(2,128)S(1)}, f32[2,256]{1,0:T(2,128)S(1)}, u32[]{:S(2)}, u32[]{:S(2)}) collective-permute-start(f32[2,256]{1,0:T(2,128)S(1)} %get-tuple-element.566), channel_id=1, source_target_pairs={{0,232},{8,240},{16,248},{24,0},{32,8},{40,16},{48,24},{56,32},{64... | collective-permute-start | bytes 6152 | tf_op jit(solution)/shard_map/while/body/eval_jaxpr/ppermute | solution.py:22
  323.9 7.3 multiply_divide_fusion.4
  331.2 8.1 %fusion.45 = f32[2,257,512]{1,0,2:T(2,128)S(1)} fusion(f32[2,256,512]{1,0,2:T(2,128)S(1)} %get-tuple-element.607, f32[2,1,512]{1,0,2:T(2,128)S(1)} %copy.143, f32[2,1,512]{1,0,2:T(2,128)S(1)} %copy-done.5, f32[2,258,514]{1,0,2:T(2,128)S(1)} %maximum_add_fusion.6, f32[2]{0:T(128)S(1)} %bitcast.105), kind=kLoop, calls=%fused_computation.10.clone.1 | loop fusion | flops 2894848 | bytes 4214792 | tf_op jit(solution)/shard_map/while/body/eval_jaxpr/div | solution.py:61
  346.2 298.3 %while.29 = (s32[]{:T(128)}, f32[2,256,512]{1,0,2:T(2,128)S(1)}, f32[2,256,512]{1,0,2:T(2,128)}, pred[]{:T(512)}, pred[]{:T(512)}, /*index=5*/f32[258,514]{0,1:T...) while((s32[]{:T(128)}, f32[2,256,512]{1,0,2:T(2,128)S(1)}, ...), condition=%wide.region_6.8_spmd, body=%wide.region_5.7_spmd.sunk | while | flops 12489274 | bytes 39043804 | solution.py:130
  346.3 7.5 collective-permute-start.8
  375.6 7.3 multiply_divide_fusion.5
  382.9 8.1 %fusion.48 = f32[2,257,512]{1,0,2:T(2,128)S(1)} fusion(f32[2,256,512]{1,0,2:T(2,128)S(1)} %get-tuple-element.646, f32[2,1,512]{1,0,2:T(2,128)S(1)} %copy-done.4, f32[2,1,512]{1,0,2:T(2,128)S(1)} %copy-done.6, f32[2,258,514]{1,0,2:T(2,128)S(1)} %maximum_add_fusion.7, f32[2]{0:T(128)S(1)} %bitcast.107), kind=kLoop, calls=%fused_computation.50.clone.1 | loop fusion | flops 2894848 | bytes 4214792 | tf_op jit(solution)/shard_map/while/body/eval_jaxpr/div | solution.py:61
  425.2 7.3 multiply_divide_fusion.5
  432.5 8.1 %fusion.48 = f32[2,257,512]{1,0,2:T(2,128)S(1)} fusion(f32[2,256,512]{1,0,2:T(2,128)S(1)} %get-tuple-element.646, f32[2,1,512]{1,0,2:T(2,128)S(1)} %copy-done.4, f32[2,1,512]{1,0,2:T(2,128)S(1)} %copy-done.6, f32[2,258,514]{1,0,2:T(2,128)S(1)} %maximum_add_fusion.7, f32[2]{0:T(128)S(1)} %bitcast.107), kind=kLoop, calls=%fused_computation.50.clone.1 | loop fusion | flops 2894848 | bytes 4214792 | tf_op jit(solution)/shard_map/while/body/eval_jaxpr/div | solution.py:61
  446.1 6.9 collective-permute-start.8
  474.8 7.3 multiply_divide_fusion.5
  482.1 8.1 %fusion.48 = f32[2,257,512]{1,0,2:T(2,128)S(1)} fusion(f32[2,256,512]{1,0,2:T(2,128)S(1)} %get-tuple-element.646, f32[2,1,512]{1,0,2:T(2,128)S(1)} %copy-done.4, f32[2,1,512]{1,0,2:T(2,128)S(1)} %copy-done.6, f32[2,258,514]{1,0,2:T(2,128)S(1)} %maximum_add_fusion.7, f32[2]{0:T(128)S(1)} %bitcast.107), kind=kLoop, calls=%fused_computation.50.clone.1 | loop fusion | flops 2894848 | bytes 4214792 | tf_op jit(solution)/shard_map/while/body/eval_jaxpr/div | solution.py:61
  524.3 7.3 multiply_divide_fusion.5
  531.6 8.1 %fusion.48 = f32[2,257,512]{1,0,2:T(2,128)S(1)} fusion(f32[2,256,512]{1,0,2:T(2,128)S(1)} %get-tuple-element.646, f32[2,1,512]{1,0,2:T(2,128)S(1)} %copy-done.4, f32[2,1,512]{1,0,2:T(2,128)S(1)} %copy-done.6, f32[2,258,514]{1,0,2:T(2,128)S(1)} %maximum_add_fusion.7, f32[2]{0:T(128)S(1)} %bitcast.107), kind=kLoop, calls=%fused_computation.50.clone.1 | loop fusion | flops 2894848 | bytes 4214792 | tf_op jit(solution)/shard_map/while/body/eval_jaxpr/div | solution.py:61
  573.9 7.3 multiply_divide_fusion.5
  581.2 8.1 %fusion.48 = f32[2,257,512]{1,0,2:T(2,128)S(1)} fusion(f32[2,256,512]{1,0,2:T(2,128)S(1)} %get-tuple-element.646, f32[2,1,512]{1,0,2:T(2,128)S(1)} %copy-done.4, f32[2,1,512]{1,0,2:T(2,128)S(1)} %copy-done.6, f32[2,258,514]{1,0,2:T(2,128)S(1)} %maximum_add_fusion.7, f32[2]{0:T(128)S(1)} %bitcast.107), kind=kLoop, calls=%fused_computation.50.clone.1 | loop fusion | flops 2894848 | bytes 4214792 | tf_op jit(solution)/shard_map/while/body/eval_jaxpr/div | solution.py:61
  623.5 7.3 multiply_divide_fusion.5
  630.8 8.1 %fusion.48 = f32[2,257,512]{1,0,2:T(2,128)S(1)} fusion(f32[2,256,512]{1,0,2:T(2,128)S(1)} %get-tuple-element.646, f32[2,1,512]{1,0,2:T(2,128)S(1)} %copy-done.4, f32[2,1,512]{1,0,2:T(2,128)S(1)} %copy-done.6, f32[2,258,514]{1,0,2:T(2,128)S(1)} %maximum_add_fusion.7, f32[2]{0:T(128)S(1)} %bitcast.107), kind=kLoop, calls=%fused_computation.50.clone.1 | loop fusion | flops 2894848 | bytes 4214792 | tf_op jit(solution)/shard_map/while/body/eval_jaxpr/div | solution.py:61
  651.8 72.8 %all-reduce = (f32[2]{0:T(128)S(1)}, f32[]{:T(128)}) all-reduce(f32[2]{0:T(128)S(1)} %add.160, f32[]{:T(128)S(6)} %mul.249), channel_id=1, replica_groups=mesh['space'=32,'dom'=8] {'space'}, use_global_device_ids=true, to_apply=%region_10.12 | all-reduce | flops 3 | bytes 24 | tf_op jit(solution)/shard_map/psum | solution.py:135
  725.9 32.4 %psum.23 = f32[]{:T(128)} all-reduce(f32[]{:T(128)} %get-tuple-element.397), channel_id=1, replica_groups=mesh['space'=32,'dom'=8] {'dom'}, use_global_device_ids=true, to_apply=%region_14.16 | all-reduce | flops 1 | bytes 8 | tf_op jit(solution)/shard_map/psum | solution.py:137
  (505 shorter events, 434.6 us)
Async XLA Ops:
  2.0 42.1 %collective-permute-start.17 = (f32[256]{0:T(256)S(1)}, f32[256]{0:T(256)S(1)}, u32[]{:S(2)}, u32[]{:S(2)}) collective-permute-start(f32[256]{0:T(256)S(1)} %bitcast.129), channel_id=1, source_target_pairs={{0,248},{8,0},{16,8},{24,16},{32,24},{40,32},{48,40},{56,48},{64,5... | collective-permute-start | bytes 3080 | tf_op jit(solution)/shard_map/ppermute | solution.py:22
  6.9 43.3 %collective-permute-start.16 = (f32[256]{0:T(256)S(1)}, f32[256]{0:T(256)S(1)}, u32[]{:S(2)}, u32[]{:S(2)}) collective-permute-start(f32[256]{0:T(256)S(1)} %bitcast.130), channel_id=1, source_target_pairs={{0,24},{8,32},{16,40},{24,48},{32,56},{40,64},{48,72},{56,80},{64,... | collective-permute-start | bytes 3080 | tf_op jit(solution)/shard_map/ppermute | solution.py:22
  6.9 43.4 %collective-permute-start.13 = (f32[256]{0:T(256)S(1)}, f32[256]{0:T(256)S(1)}, u32[]{:S(2)}, u32[]{:S(2)}) collective-permute-start(f32[256]{0:T(256)S(1)} %bitcast.127), channel_id=1, source_target_pairs={{0,8},{8,16},{16,24},{24,32},{32,40},{40,48},{48,56},{56,64},{64,7... | collective-permute-start | bytes 3080 | tf_op jit(solution)/shard_map/ppermute | solution.py:22
  6.9 43.4 %collective-permute-start.12 = (f32[256]{0:T(256)S(1)}, f32[256]{0:T(256)S(1)}, u32[]{:S(2)}, u32[]{:S(2)}) collective-permute-start(f32[256]{0:T(256)S(1)} %bitcast.128), channel_id=1, source_target_pairs={{0,232},{8,240},{16,248},{24,0},{32,8},{40,16},{48,24},{56,32},{64... | collective-permute-start | bytes 3080 | tf_op jit(solution)/shard_map/ppermute | solution.py:22
  14.8 39.8 %all-to-all-start = ((bf16[8,2,2,1,32,512]{5,4,3,2,1,0:T(8,128)(2,1)}), bf16[8,2,2,1,32,512]{5,4,3,2,1,0:T(8,128)(2,1)}, u32[]{:S(2)}, u32[]{:S(2)}) async-start(bf16[8,2,2,1,32,512]{5,4,3,2,1,0:T(8,128)(2,1)} %stack.2), calls=%async_computation | async-start | bytes 2097152 | tf_op jit(solution)/shard_map/all_to_all | solution.py:115
  60.2 18.8 %collective-permute-start.2 = (f32[2,256]{1,0:T(2,128)S(1)}, f32[2,256]{1,0:T(2,128)S(1)}, u32[]{:S(2)}, u32[]{:S(2)}) collective-permute-start(f32[2,256]{1,0:T(2,128)S(1)} %get-tuple-element.566), channel_id=1, source_target_pairs={{0,232},{8,240},{16,248},{24,0},{32,8},{40,16},{48,24},{56,32},{64... | collective-permute-start | bytes 6152 | tf_op jit(solution)/shard_map/while/body/eval_jaxpr/ppermute | solution.py:22
  63.5 15.5 %collective-permute-start.5 = (f32[2,256]{1,0:T(2,128)S(1)}, f32[2,256]{1,0:T(2,128)S(1)}, u32[]{:S(2)}, u32[]{:S(2)}) collective-permute-start(f32[2,256]{1,0:T(2,128)S(1)} %get-tuple-element.567), channel_id=1, source_target_pairs={{0,248},{8,0},{16,8},{24,16},{32,24},{40,32},{48,40},{56,48},{64,5... | collective-permute-start | bytes 6152 | tf_op jit(solution)/shard_map/while/body/eval_jaxpr/ppermute | solution.py:22
  107.5 18.8 %collective-permute-start.2 = (f32[2,256]{1,0:T(2,128)S(1)}, f32[2,256]{1,0:T(2,128)S(1)}, u32[]{:S(2)}, u32[]{:S(2)}) collective-permute-start(f32[2,256]{1,0:T(2,128)S(1)} %get-tuple-element.566), channel_id=1, source_target_pairs={{0,232},{8,240},{16,248},{24,0},{32,8},{40,16},{48,24},{56,32},{64... | collective-permute-start | bytes 6152 | tf_op jit(solution)/shard_map/while/body/eval_jaxpr/ppermute | solution.py:22
  111.0 15.3 %collective-permute-start.5 = (f32[2,256]{1,0:T(2,128)S(1)}, f32[2,256]{1,0:T(2,128)S(1)}, u32[]{:S(2)}, u32[]{:S(2)}) collective-permute-start(f32[2,256]{1,0:T(2,128)S(1)} %get-tuple-element.567), channel_id=1, source_target_pairs={{0,248},{8,0},{16,8},{24,16},{32,24},{40,32},{48,40},{56,48},{64,5... | collective-permute-start | bytes 6152 | tf_op jit(solution)/shard_map/while/body/eval_jaxpr/ppermute | solution.py:22
  154.7 18.8 %collective-permute-start.2 = (f32[2,256]{1,0:T(2,128)S(1)}, f32[2,256]{1,0:T(2,128)S(1)}, u32[]{:S(2)}, u32[]{:S(2)}) collective-permute-start(f32[2,256]{1,0:T(2,128)S(1)} %get-tuple-element.566), channel_id=1, source_target_pairs={{0,232},{8,240},{16,248},{24,0},{32,8},{40,16},{48,24},{56,32},{64... | collective-permute-start | bytes 6152 | tf_op jit(solution)/shard_map/while/body/eval_jaxpr/ppermute | solution.py:22
  158.9 14.7 %collective-permute-start.5 = (f32[2,256]{1,0:T(2,128)S(1)}, f32[2,256]{1,0:T(2,128)S(1)}, u32[]{:S(2)}, u32[]{:S(2)}) collective-permute-start(f32[2,256]{1,0:T(2,128)S(1)} %get-tuple-element.567), channel_id=1, source_target_pairs={{0,248},{8,0},{16,8},{24,16},{32,24},{40,32},{48,40},{56,48},{64,5... | collective-permute-start | bytes 6152 | tf_op jit(solution)/shard_map/while/body/eval_jaxpr/ppermute | solution.py:22
  201.9 18.8 %collective-permute-start.2 = (f32[2,256]{1,0:T(2,128)S(1)}, f32[2,256]{1,0:T(2,128)S(1)}, u32[]{:S(2)}, u32[]{:S(2)}) collective-permute-start(f32[2,256]{1,0:T(2,128)S(1)} %get-tuple-element.566), channel_id=1, source_target_pairs={{0,232},{8,240},{16,248},{24,0},{32,8},{40,16},{48,24},{56,32},{64... | collective-permute-start | bytes 6152 | tf_op jit(solution)/shard_map/while/body/eval_jaxpr/ppermute | solution.py:22
  206.5 14.3 %collective-permute-start.5 = (f32[2,256]{1,0:T(2,128)S(1)}, f32[2,256]{1,0:T(2,128)S(1)}, u32[]{:S(2)}, u32[]{:S(2)}) collective-permute-start(f32[2,256]{1,0:T(2,128)S(1)} %get-tuple-element.567), channel_id=1, source_target_pairs={{0,248},{8,0},{16,8},{24,16},{32,24},{40,32},{48,40},{56,48},{64,5... | collective-permute-start | bytes 6152 | tf_op jit(solution)/shard_map/while/body/eval_jaxpr/ppermute | solution.py:22
  249.2 18.8 %collective-permute-start.2 = (f32[2,256]{1,0:T(2,128)S(1)}, f32[2,256]{1,0:T(2,128)S(1)}, u32[]{:S(2)}, u32[]{:S(2)}) collective-permute-start(f32[2,256]{1,0:T(2,128)S(1)} %get-tuple-element.566), channel_id=1, source_target_pairs={{0,232},{8,240},{16,248},{24,0},{32,8},{40,16},{48,24},{56,32},{64... | collective-permute-start | bytes 6152 | tf_op jit(solution)/shard_map/while/body/eval_jaxpr/ppermute | solution.py:22
  296.4 14.0 %collective-permute-start.3 = (f32[2,256]{1,0:T(2,128)S(1)}, f32[2,256]{1,0:T(2,128)S(1)}, u32[]{:S(2)}, u32[]{:S(2)}) collective-permute-start(f32[2,256]{1,0:T(2,128)S(1)} %get-tuple-element.566), channel_id=1, source_target_pairs={{0,8},{8,16},{16,24},{24,32},{32,40},{40,48},{48,56},{56,64},{64,7... | collective-permute-start | bytes 6152 | tf_op jit(solution)/shard_map/while/body/eval_jaxpr/ppermute | solution.py:22
  296.4 20.0 %collective-permute-start.2 = (f32[2,256]{1,0:T(2,128)S(1)}, f32[2,256]{1,0:T(2,128)S(1)}, u32[]{:S(2)}, u32[]{:S(2)}) collective-permute-start(f32[2,256]{1,0:T(2,128)S(1)} %get-tuple-element.566), channel_id=1, source_target_pairs={{0,232},{8,240},{16,248},{24,0},{32,8},{40,16},{48,24},{56,32},{64... | collective-permute-start | bytes 6152 | tf_op jit(solution)/shard_map/while/body/eval_jaxpr/ppermute | solution.py:22
  346.2 15.0 %collective-permute-start.9 = (f32[2,256]{1,0:T(2,128)S(1)}, f32[2,256]{1,0:T(2,128)S(1)}, u32[]{:S(2)}, u32[]{:S(2)}) collective-permute-start(f32[2,256]{1,0:T(2,128)S(1)} %get-tuple-element.586), channel_id=1, source_target_pairs={{0,8},{8,16},{16,24},{24,32},{32,40},{40,48},{48,56},{56,64},{64,7... | collective-permute-start | bytes 6152 | tf_op jit(solution)/shard_map/while/body/eval_jaxpr/ppermute | solution.py:22
  346.3 20.9 %collective-permute-start.8 = (f32[2,256]{1,0:T(2,128)S(1)}, f32[2,256]{1,0:T(2,128)S(1)}, u32[]{:S(2)}, u32[]{:S(2)}) collective-permute-start(f32[2,256]{1,0:T(2,128)S(1)} %get-tuple-element.586), channel_id=1, source_target_pairs={{0,232},{8,240},{16,248},{24,0},{32,8},{40,16},{48,24},{56,32},{64... | collective-permute-start | bytes 6152 | tf_op jit(solution)/shard_map/while/body/eval_jaxpr/ppermute | solution.py:22
  353.8 13.5 %collective-permute-start.11 = (f32[2,256]{1,0:T(2,128)S(1)}, f32[2,256]{1,0:T(2,128)S(1)}, u32[]{:S(2)}, u32[]{:S(2)}) collective-permute-start(f32[2,256]{1,0:T(2,128)S(1)} %get-tuple-element.587), channel_id=1, source_target_pairs={{0,248},{8,0},{16,8},{24,16},{32,24},{40,32},{48,40},{56,48},{64,5... | collective-permute-start | bytes 6152 | tf_op jit(solution)/shard_map/while/body/eval_jaxpr/ppermute | solution.py:22
  396.6 14.1 %collective-permute-start.9 = (f32[2,256]{1,0:T(2,128)S(1)}, f32[2,256]{1,0:T(2,128)S(1)}, u32[]{:S(2)}, u32[]{:S(2)}) collective-permute-start(f32[2,256]{1,0:T(2,128)S(1)} %get-tuple-element.586), channel_id=1, source_target_pairs={{0,8},{8,16},{16,24},{24,32},{32,40},{40,48},{48,56},{56,64},{64,7... | collective-permute-start | bytes 6152 | tf_op jit(solution)/shard_map/while/body/eval_jaxpr/ppermute | solution.py:22
  396.6 20.2 %collective-permute-start.8 = (f32[2,256]{1,0:T(2,128)S(1)}, f32[2,256]{1,0:T(2,128)S(1)}, u32[]{:S(2)}, u32[]{:S(2)}) collective-permute-start(f32[2,256]{1,0:T(2,128)S(1)} %get-tuple-element.586), channel_id=1, source_target_pairs={{0,232},{8,240},{16,248},{24,0},{32,8},{40,16},{48,24},{56,32},{64... | collective-permute-start | bytes 6152 | tf_op jit(solution)/shard_map/while/body/eval_jaxpr/ppermute | solution.py:22
  403.4 13.4 %collective-permute-start.10 = (f32[2,256]{1,0:T(2,128)S(1)}, f32[2,256]{1,0:T(2,128)S(1)}, u32[]{:S(2)}, u32[]{:S(2)}) collective-permute-start(f32[2,256]{1,0:T(2,128)S(1)} %get-tuple-element.587), channel_id=1, source_target_pairs={{0,24},{8,32},{16,40},{24,48},{32,56},{40,64},{48,72},{56,80},{64,... | collective-permute-start | bytes 6152 | tf_op jit(solution)/shard_map/while/body/eval_jaxpr/ppermute | solution.py:22
  446.1 14.2 %collective-permute-start.9 = (f32[2,256]{1,0:T(2,128)S(1)}, f32[2,256]{1,0:T(2,128)S(1)}, u32[]{:S(2)}, u32[]{:S(2)}) collective-permute-start(f32[2,256]{1,0:T(2,128)S(1)} %get-tuple-element.586), channel_id=1, source_target_pairs={{0,8},{8,16},{16,24},{24,32},{32,40},{40,48},{48,56},{56,64},{64,7... | collective-permute-start | bytes 6152 | tf_op jit(solution)/shard_map/while/body/eval_jaxpr/ppermute | solution.py:22
  446.1 20.2 %collective-permute-start.8 = (f32[2,256]{1,0:T(2,128)S(1)}, f32[2,256]{1,0:T(2,128)S(1)}, u32[]{:S(2)}, u32[]{:S(2)}) collective-permute-start(f32[2,256]{1,0:T(2,128)S(1)} %get-tuple-element.586), channel_id=1, source_target_pairs={{0,232},{8,240},{16,248},{24,0},{32,8},{40,16},{48,24},{56,32},{64... | collective-permute-start | bytes 6152 | tf_op jit(solution)/shard_map/while/body/eval_jaxpr/ppermute | solution.py:22
  453.0 13.4 %collective-permute-start.10 = (f32[2,256]{1,0:T(2,128)S(1)}, f32[2,256]{1,0:T(2,128)S(1)}, u32[]{:S(2)}, u32[]{:S(2)}) collective-permute-start(f32[2,256]{1,0:T(2,128)S(1)} %get-tuple-element.587), channel_id=1, source_target_pairs={{0,24},{8,32},{16,40},{24,48},{32,56},{40,64},{48,72},{56,80},{64,... | collective-permute-start | bytes 6152 | tf_op jit(solution)/shard_map/while/body/eval_jaxpr/ppermute | solution.py:22
  495.7 14.2 %collective-permute-start.9 = (f32[2,256]{1,0:T(2,128)S(1)}, f32[2,256]{1,0:T(2,128)S(1)}, u32[]{:S(2)}, u32[]{:S(2)}) collective-permute-start(f32[2,256]{1,0:T(2,128)S(1)} %get-tuple-element.586), channel_id=1, source_target_pairs={{0,8},{8,16},{16,24},{24,32},{32,40},{40,48},{48,56},{56,64},{64,7... | collective-permute-start | bytes 6152 | tf_op jit(solution)/shard_map/while/body/eval_jaxpr/ppermute | solution.py:22
  495.7 20.2 %collective-permute-start.8 = (f32[2,256]{1,0:T(2,128)S(1)}, f32[2,256]{1,0:T(2,128)S(1)}, u32[]{:S(2)}, u32[]{:S(2)}) collective-permute-start(f32[2,256]{1,0:T(2,128)S(1)} %get-tuple-element.586), channel_id=1, source_target_pairs={{0,232},{8,240},{16,248},{24,0},{32,8},{40,16},{48,24},{56,32},{64... | collective-permute-start | bytes 6152 | tf_op jit(solution)/shard_map/while/body/eval_jaxpr/ppermute | solution.py:22
  502.6 13.4 %collective-permute-start.10 = (f32[2,256]{1,0:T(2,128)S(1)}, f32[2,256]{1,0:T(2,128)S(1)}, u32[]{:S(2)}, u32[]{:S(2)}) collective-permute-start(f32[2,256]{1,0:T(2,128)S(1)} %get-tuple-element.587), channel_id=1, source_target_pairs={{0,24},{8,32},{16,40},{24,48},{32,56},{40,64},{48,72},{56,80},{64,... | collective-permute-start | bytes 6152 | tf_op jit(solution)/shard_map/while/body/eval_jaxpr/ppermute | solution.py:22
  545.3 14.2 %collective-permute-start.9 = (f32[2,256]{1,0:T(2,128)S(1)}, f32[2,256]{1,0:T(2,128)S(1)}, u32[]{:S(2)}, u32[]{:S(2)}) collective-permute-start(f32[2,256]{1,0:T(2,128)S(1)} %get-tuple-element.586), channel_id=1, source_target_pairs={{0,8},{8,16},{16,24},{24,32},{32,40},{40,48},{48,56},{56,64},{64,7... | collective-permute-start | bytes 6152 | tf_op jit(solution)/shard_map/while/body/eval_jaxpr/ppermute | solution.py:22
  545.3 20.2 %collective-permute-start.8 = (f32[2,256]{1,0:T(2,128)S(1)}, f32[2,256]{1,0:T(2,128)S(1)}, u32[]{:S(2)}, u32[]{:S(2)}) collective-permute-start(f32[2,256]{1,0:T(2,128)S(1)} %get-tuple-element.586), channel_id=1, source_target_pairs={{0,232},{8,240},{16,248},{24,0},{32,8},{40,16},{48,24},{56,32},{64... | collective-permute-start | bytes 6152 | tf_op jit(solution)/shard_map/while/body/eval_jaxpr/ppermute | solution.py:22
  594.9 14.2 %collective-permute-start.9 = (f32[2,256]{1,0:T(2,128)S(1)}, f32[2,256]{1,0:T(2,128)S(1)}, u32[]{:S(2)}, u32[]{:S(2)}) collective-permute-start(f32[2,256]{1,0:T(2,128)S(1)} %get-tuple-element.586), channel_id=1, source_target_pairs={{0,8},{8,16},{16,24},{24,32},{32,40},{40,48},{48,56},{56,64},{64,7... | collective-permute-start | bytes 6152 | tf_op jit(solution)/shard_map/while/body/eval_jaxpr/ppermute | solution.py:22
  594.9 20.2 %collective-permute-start.8 = (f32[2,256]{1,0:T(2,128)S(1)}, f32[2,256]{1,0:T(2,128)S(1)}, u32[]{:S(2)}, u32[]{:S(2)}) collective-permute-start(f32[2,256]{1,0:T(2,128)S(1)} %get-tuple-element.586), channel_id=1, source_target_pairs={{0,232},{8,240},{16,248},{24,0},{32,8},{40,16},{48,24},{56,32},{64... | collective-permute-start | bytes 6152 | tf_op jit(solution)/shard_map/while/body/eval_jaxpr/ppermute | solution.py:22
  (118 other events, 941.3 us)
